TPU v7x, 32 devices: a whole 2x2x4 slice. The times are simulated.
32 devices in a mesh: row: 4 (over y, core), col: 8 (over z, x).
Axes of the slice: x: 2, y: 2, z: 4, core: 2. Of those that a mesh axis runs over, the one named last changes fastest.
Arguments:
- acts: bfloat16 [192, 2, 28672], P('col', None, 'row'), may hold values from -6 to 6
- grads: bfloat16 [192, 2, 8192], P('row', None, 'col'), may hold values from -0.3984375 to 0.3984375
- basis_in: bfloat16 [28672, 28672], P('row', 'col'), may hold values from -0.03125 to 0.03125
- basis_out: bfloat16 [8192, 8192], P('col', 'row'), may hold values from -0.0625 to 0.0625
- eigen: bfloat16 [28672, 8192], P('col', 'row'), may hold values from 0.5 to 8
- sketch: bfloat16 [72, 8192], P(None, 'col'), may hold values from -0.0625 to 0.0625
Outputs:
- range_basis: float32 [2, 72, 28672], P(None, None, 'row')
- projected: float32 [2, 72, 8192], P(None, None, 'col')
All inputs are finite; a program needn't handle non-finite values.
Results may differ from a plain program's by a relative error of at most 0.018.
Values may be sent and summed in bfloat16 or wider, within the bound.
A program may use at most 192 MiB of HBM per device.

v0:
```python
import jax
import jax.numpy as jnp
from jax import lax
from jax.sharding import PartitionSpec as P


def on_device(acts, grads, basis_in, basis_out, eigen, sketch):
    full_acts = lax.all_gather(acts, "col", axis=0, tiled=True)
    rows = full_acts
    act_shares = lax.psum_scatter(
        jnp.einsum("tqi,ij->tqj", rows, basis_in, preferred_element_type=jnp.float32),
        "row",
        scatter_dimension=0,
        tiled=True,
    ).astype(jnp.bfloat16)
    full_grads = lax.all_gather(grads, "row", axis=0, tiled=True)
    tokens = full_grads.shape[0]
    queries = full_grads.shape[1]
    flat_grads = full_grads.reshape(tokens * queries, full_grads.shape[2])
    joined = jnp.concatenate([flat_grads, sketch], axis=0)
    joined_sum = lax.psum(
        jnp.dot(joined, basis_out, preferred_element_type=jnp.float32), "col"
    ).astype(jnp.bfloat16)
    grad_rot = joined_sum[: tokens * queries].reshape(tokens, queries, basis_out.shape[1])
    sketch_rot = joined_sum[tokens * queries :]
    rows = grad_rot
    core_sum = jnp.einsum(
        "tqj,tqp->qjp",
        lax.all_gather(act_shares, "row", axis=0, tiled=True),
        rows,
        preferred_element_type=jnp.float32,
    )
    scaled = (core_sum / eigen.astype(jnp.float32)).astype(jnp.bfloat16)
    reduced_part = jnp.einsum("qjp,sp->qsj", scaled, sketch_rot, preferred_element_type=jnp.float32)
    reduced = lax.psum(reduced_part, "row").astype(jnp.bfloat16)
    range_part = jnp.einsum("qsj,ij->qsi", reduced, basis_in, preferred_element_type=jnp.float32)
    range_rows = lax.psum(range_part, "col")
    gram_piece = jnp.einsum("qsi,qri->qsr", range_rows, range_rows, precision=lax.Precision.HIGHEST)
    gram = lax.psum(gram_piece, "row")
    factor = jnp.linalg.cholesky(gram)
    basis_rows = lax.linalg.triangular_solve(factor, range_rows, left_side=True, lower=True)
    mapped_part = jnp.einsum(
        "qsi,ij->qsj", basis_rows.astype(jnp.bfloat16), basis_in, preferred_element_type=jnp.float32
    )
    mapped = lax.psum(mapped_part.astype(jnp.bfloat16), "row")
    core_part = jnp.einsum("qsj,qjp->qsp", mapped, scaled, preferred_element_type=jnp.float32)
    core = lax.psum(core_part.astype(jnp.bfloat16), "col")
    projection_part = jnp.einsum("qsp,op->qso", core, basis_out, preferred_element_type=jnp.float32)
    projected = lax.psum(projection_part.astype(jnp.bfloat16), "row").astype(jnp.float32)
    return (basis_rows, projected)


def solution(mesh):
    in_specs = (
        P("col", None, "row"),
        P("row", None, "col"),
        P("row", "col"),
        P("col", "row"),
        P("col", "row"),
        P(None, "col"),
    )
    out_specs = (P(None, None, "row"), P(None, None, "col"))
    return jax.shard_map(
        on_device, mesh=mesh, in_specs=in_specs, out_specs=out_specs, check_vma=False
    )
```

profile of v0, /device:TPU:0, one launch (start us, length us, event | category | flops | bytes accessed | tf_op | source)
XLA Modules:
  0.0 866.9 jit_solution(3863842434083049462)
XLA Ops:
  7.2 0.7 all-gather.3.cloned.1.call-update
  7.9 94.1 %all-gather.3.cloned.1.call-done = bf16[192,2,7168]{2,1,0:T(2,128)(2,1)} async-done(((bf16[24,2,7168]{2,1,0:T(2,128)(2,1)}), bf16[192,2,7168]{2,1,0:T(2,128)(2,1)}) %all-gather.3.cloned.1.call-update) | async-done | bytes 5505040 | tf_op jit(solution)/shard_map/all_gather | solution.py:8
  102.0 30.9 %fusion.4 = f32[192,2,3584]{2,0,1:T(8,128)} fusion(bf16[7168,3584]{1,0:T(8,128)(2,1)} %param.8, bf16[192,2,7168]{2,1,0:T(2,128)(2,1)} %all-gather.3.cloned.1.call-done), kind=kOutput, calls=%fused_computation.5 | convolution fusion | flops 19730006016 | bytes 62390272 | tf_op jit(solution)/shard_map/tqi,ij->tqj/dot_general | solution.py:11
  133.0 51.3 %reduce-scatter.2.cloned.1.call-done = f32[48,2,3584]{2,0,1:T(8,128)} async-done(((f32[192,2,3584]{2,0,1:T(8,128)}), f32[48,2,3584]{2,0,1:T(8,128)}) %reduce-scatter.2.cloned.1.call-update) | async-done | bytes 1376272 | tf_op jit(solution)/shard_map/reduce_scatter | solution.py:10
  184.3 2.3 convert_element_type.31
  186.7 8.0 all_gather.9
  194.7 0.3 reshape.21
  195.0 6.2 fusion.18
  201.2 150.4 %all-reduce.14 = bf16[456,2048]{1,0:T(8,128)(2,1)S(1)} all-reduce(f32[456,2048]{1,0:T(8,128)} %fusion.18), channel_id=1, replica_groups=mesh['row'=4,'col'=8] {'col'}, use_global_device_ids=true, to_apply=%region_0.0 | all-reduce | flops 933888 | bytes 5603328 | tf_op jit(solution)/shard_map/psum | solution.py:21
  351.6 0.2 slice.19
  351.8 2.4 reshape.22
  354.1 16.6 %convert_element_type.32 = f32[3584,2048]{1,0:T(8,128)} convert(bf16[3584,2048]{1,0:T(8,128)(2,1)} %param.10) | non-fusion elementwise | flops 7340032 | bytes 44040192 | tf_op jit(solution)/shard_map/convert_element_type | solution.py:33
  370.8 22.4 %divide_convert_fusion = bf16[2,3584,2048]{2,1,0:T(8,128)(2,1)} fusion(f32[3584,2048]{1,0:T(8,128)} %convert_element_type.32, bf16[192,2,3584]{2,0,1:T(8,128)(2,1)} %all-gather.5.cloned.1.call-done, bf16[192,2,2048]{2,1,0:T(2,128)(2,1)S(1)} %copy-done.2), kind=kOutput, calls=%fused_computation | convolution fusion | flops 5666504704 | bytes 63045632 | tf_op jit(solution)/shard_map/tqj,tqp->qjp/dot_general | solution.py:27
  393.2 14.3 %convolution_bitcast_fusion = f32[2,72,3584]{2,1,0:T(8,128)S(1)} fusion(bf16[2,3584,2048]{2,1,0:T(8,128)(2,1)} %divide_convert_fusion, bf16[456,2048]{1,0:T(8,128)(2,1)} %copy-done.1), kind=kOutput, calls=%fused_computation.8 | convolution fusion | flops 2113929216 | bytes 31719424 | tf_op jit(solution)/shard_map/qjp,sp->qsj/dot_general | solution.py:34
  407.5 39.8 %all-reduce.15 = bf16[2,72,3584]{2,1,0:T(8,128)(2,1)S(1)} all-reduce(f32[2,72,3584]{2,1,0:T(8,128)S(1)} %convolution_bitcast_fusion), channel_id=1, replica_groups=mesh['row'=4,'col'=8] {'row'}, use_global_device_ids=true, to_apply=%region_2.0 | all-reduce | flops 516096 | bytes 3096576 | tf_op jit(solution)/shard_map/psum | solution.py:35
  447.3 26.5 %fusion.2 = f32[2,72,7168]{2,1,0:T(8,128)} fusion(bf16[7168,3584]{1,0:T(8,128)(2,1)} %param.8, bf16[2,72,3584]{2,1,0:T(8,128)(2,1)S(1)} %all-reduce.15), kind=kOutput, calls=%fused_computation.3 | convolution fusion | flops 7398752256 | bytes 56541184 | tf_op jit(solution)/shard_map/qsj,ij->qsi/dot_general | solution.py:36
  473.9 0.3 all-reduce.9.cloned.1.call-start
  474.2 153.0 %all-reduce.7.cloned.1.call-done = f32[2,72,7168]{2,1,0:T(8,128)} async-done(((f32[2,72,7168]{2,1,0:T(8,128)}), f32[2,72,7168]{2,1,0:T(8,128)}) %all-reduce.7.cloned.1.call-update) | async-done | bytes 4128784 | tf_op jit(solution)/shard_map/psum | solution.py:37
  627.2 7.4 fusion.26
  634.6 12.0 %psum.52 = f32[2,72,72]{1,2,0:T(8,128)S(1)} all-reduce(f32[2,72,72]{1,2,0:T(8,128)S(1)} %fusion.26), channel_id=1, replica_groups=mesh['row'=4,'col'=8] {'row'}, use_global_device_ids=true, to_apply=%region_4.0 | all-reduce | flops 10368 | bytes 82944 | tf_op jit(solution)/shard_map/psum | solution.py:39
  646.7 13.2 %custom-call.7 = f32[2,72,72]{2,1,0:T(8,128)S(1)} custom-call(f32[2,72,72]{2,1,0:T(8,128)S(1)} %fusion.24), custom_call_target="Cholesky" | custom-call | tf_op jit(solution)/shard_map/jit(cholesky)/cholesky | solution.py:40
  660.2 11.1 %custom-call.8 = f32[2,1,72,72]{2,3,1,0:T(8,128)S(1)} custom-call(f32[2,1,72,72]{3,2,1,0:T(8,128)S(1)} %select_bitcast_fusion), custom_call_target="InvertDiagBlocksLowerTriangular" | custom-call | tf_op jit(solution)/shard_map/triangular_solve | solution.py:41
  671.3 5.3 fusion.22
  676.6 2.0 copy-done
  678.6 19.0 %fusion.7 = bf16[2,72,3584]{2,1,0:T(8,128)(2,1)} fusion(bf16[7168,3584]{1,0:T(8,128)(2,1)} %param.8, f32[2,72,7168]{2,1,0:T(8,128)S(1)} %fusion.22), kind=kOutput, calls=%fused_computation.9 | convolution fusion | flops 7400300544 | bytes 56541184 | tf_op jit(solution)/shard_map/qsi,ij->qsj/dot_general | solution.py:42
  697.7 0.3 all-reduce.11.cloned.1.call-start
  698.0 34.3 %all-reduce.9.cloned.1.call-done = bf16[2,72,3584]{2,1,0:T(8,128)(2,1)} async-done(((bf16[2,72,3584]{2,1,0:T(8,128)(2,1)}), bf16[2,72,3584]{2,1,0:T(8,128)(2,1)}) %all-reduce.9.cloned.1.call-update) | async-done | bytes 1032208 | tf_op jit(solution)/shard_map/psum | solution.py:45
  732.3 15.7 %convolution_convert_fusion = bf16[2,72,2048]{2,1,0:T(8,128)(2,1)} fusion(bf16[2,72,3584]{2,1,0:T(8,128)(2,1)} %all-reduce.9.cloned.1.call-done, bf16[2,3584,2048]{2,1,0:T(8,128)(2,1)} %divide_convert_fusion), kind=kOutput, calls=%fused_computation.12 | convolution fusion | flops 2114224128 | bytes 30982144 | tf_op jit(solution)/shard_map/qsj,qjp->qsp/dot_general | solution.py:46
  748.0 74.0 %all-reduce.11.cloned.1.call-done = bf16[2,72,2048]{2,1,0:T(8,128)(2,1)} async-done(((bf16[2,72,2048]{2,1,0:T(8,128)(2,1)}), bf16[2,72,2048]{2,1,0:T(8,128)(2,1)}) %all-reduce.11.cloned.1.call-update) | async-done | bytes 589840 | tf_op jit(solution)/shard_map/psum | solution.py:47
  822.0 4.6 fusion.14
  826.7 31.5 %all-reduce.13.cloned.1.call-done = bf16[2,72,1024]{2,1,0:T(8,128)(2,1)} async-done(((bf16[2,72,1024]{2,1,0:T(8,128)(2,1)}), bf16[2,72,1024]{2,1,0:T(8,128)(2,1)}) %all-reduce.13.cloned.1.call-update) | async-done | bytes 294928 | tf_op jit(solution)/shard_map/psum | solution.py:49
  858.2 1.8 convert_element_type.39
  (28 shorter events, 0.7 us)
Async XLA Ops:
  7.2 94.9 %all-gather.3.cloned.1.call-start = ((), (), s32[]{:S(2)}) async-start(), calls=%async_computation.1 | async-start | bytes 6193152 | tf_op jit(solution)/shard_map/all_gather | solution.py:8
  7.9 176.4 %reduce-scatter.2.cloned.1.call-start = ((), (), s32[]{:S(2)}) async-start(), calls=%async_computation.2 | async-start | bytes 6881280 | tf_op jit(solution)/shard_map/reduce_scatter | solution.py:10
  133.0 53.7 %copy-start.3 = (bf16[48,2,1024]{2,1,0:T(2,128)(2,1)S(1)}, bf16[48,2,1024]{2,1,0:T(2,128)(2,1)}, u32[]{:S(2)}) copy-start(bf16[48,2,1024]{2,1,0:T(2,128)(2,1)} %param.7) | copy-start | bytes 589828
  133.0 62.0 %copy-start.4 = (bf16[72,1024]{1,0:T(8,128)(2,1)S(1)}, bf16[72,1024]{1,0:T(8,128)(2,1)}, u32[]{:S(2)}) copy-start(bf16[72,1024]{1,0:T(8,128)(2,1)} %param.11) | copy-start | bytes 442372
  133.0 237.8 %all-gather.5.cloned.1.call-start = ((), (), s32[]{:S(2)}) async-start(), calls=%async_computation.3 | async-start | bytes 3440640 | tf_op jit(solution)/shard_map/all_gather | solution.py:29
  186.6 440.6 %all-reduce.7.cloned.1.call-start = ((), (), s32[]{:S(2)}) async-start(), calls=%async_computation.4 | async-start | bytes 8257536 | tf_op jit(solution)/shard_map/psum | solution.py:37
  351.6 19.2 %copy-start.1 = (bf16[456,2048]{1,0:T(8,128)(2,1)}, bf16[456,2048]{1,0:T(8,128)(2,1)S(1)}, u32[]{:S(2)}) copy-start(bf16[456,2048]{1,0:T(8,128)(2,1)S(1)} %all-reduce.14) | copy-start | bytes 5603332
  354.1 16.6 %copy-start.2 = (bf16[192,2,2048]{2,1,0:T(2,128)(2,1)S(1)}, bf16[192,2,2048]{2,1,0:T(2,128)(2,1)}, u32[]{:S(2)}) copy-start(bf16[192,2,2048]{2,1,0:T(2,128)(2,1)} %reshape.22) | copy-start | bytes 4718596
  473.9 258.4 %all-reduce.9.cloned.1.call-start = ((), (), s32[]{:S(2)}) async-start(), calls=%async_computation.5 | async-start | bytes 2064384 | tf_op jit(solution)/shard_map/psum | solution.py:45
  676.6 2.0 copy-start
  697.7 124.4 %all-reduce.11.cloned.1.call-start = ((), (), s32[]{:S(2)}) async-start(), calls=%async_computation.6 | async-start | bytes 1179648 | tf_op jit(solution)/shard_map/psum | solution.py:47
  748.0 110.2 %all-reduce.13.cloned.1.call-start = ((), (), s32[]{:S(2)}) async-start(), calls=%async_computation.7 | async-start | bytes 589824 | tf_op jit(solution)/shard_map/psum | solution.py:49
Sparse Core Ops, SparseCore 0:
  10.2 91.8 all-gather.2
  133.1 51.1 reduce-scatter.1
  186.7 26.2 all-gather.4
  474.0 153.1 all-reduce.6
  697.8 34.4 all-reduce.8
  748.1 73.8 all-reduce.10
  826.8 31.3 all-reduce.12
where the time goes:
time: 867 us
  waiting for transfers between devices  439 us (51%)
  blocking collectives  210 us (24%)
  matrix products  153 us (18%)
  other arithmetic  45.3 us (5%)
  between operations  14.3 us (2%)
    psum x1, waiting for transfers between devices, on_device(): range_rows = lax.psum(range_part, 'col')  153 us
    psum x1, blocking collectives, on_device(): lax.psum(jnp.dot(joined, basis_out, preferred_element_type=jnp.float32),...  150 us
    all_gather x1, waiting for transfers between devices, on_device(): full_acts = lax.all_gather(acts, 'col', axis=0, tiled=True)  94.1 us
    psum x1, waiting for transfers between devices, on_device(): core = lax.psum(core_part.astype(jnp.bfloat16), 'col')  74 us
    reduce_scatter x1, waiting for transfers between devices, on_device(): lax.psum_scatter(jnp.einsum('tqi,ij->tqj', rows, basis_in, preferred_elem...  51.3 us
    psum x1, blocking collectives, on_device(): reduced = lax.psum(reduced_part, 'row').astype(jnp.bfloat16)  39.8 us
    psum x1, waiting for transfers between devices, on_device(): mapped = lax.psum(mapped_part.astype(jnp.bfloat16), 'row')  34.3 us
    psum x1, waiting for transfers between devices, on_device(): lax.psum(projection_part.astype(jnp.bfloat16), 'row').astype(jnp.float32)  31.5 us
  transfers between devices with their start and end apart: 7, of which 6 were waited for; matrix products, arithmetic and copies ran while one was open for 3% of the time, Pallas kernels for 0%

commit v1 on v0

--- a/solution.py
+++ b/solution.py
@@ -2,6 +2,14 @@
 import jax.numpy as jnp
 from jax import lax
 from jax.sharding import PartitionSpec as P
+
+
+def sum_by_hops(shard, axis):
+    peers, total = (lax.axis_size(axis), shard)
+    for stride in [1 << k for k in range(peers.bit_length() - 1)]:
+        swap = [(i, i ^ stride) for i in range(peers)]
+        total = total + lax.ppermute(total, axis, swap)
+    return total
 
 
 def on_device(acts, grads, basis_in, basis_out, eigen, sketch):
@@ -34,7 +42,7 @@
     reduced_part = jnp.einsum("qjp,sp->qsj", scaled, sketch_rot, preferred_element_type=jnp.float32)
     reduced = lax.psum(reduced_part, "row").astype(jnp.bfloat16)
     range_part = jnp.einsum("qsj,ij->qsi", reduced, basis_in, preferred_element_type=jnp.float32)
-    range_rows = lax.psum(range_part, "col")
+    range_rows = sum_by_hops(range_part, "col")
     gram_piece = jnp.einsum("qsi,qri->qsr", range_rows, range_rows, precision=lax.Precision.HIGHEST)
     gram = lax.psum(gram_piece, "row")
     factor = jnp.linalg.cholesky(gram)

time: 867 us -> 1080 us (1.25)
  waiting for transfers between devices: 439 us -> 647 us
    ppermute x0 -> x3, waiting for transfers between devices: none -> 361 us  [sum_by_hops(): total = total + lax.ppermute(total, axis, swap)]
    psum x1 -> x0, waiting for transfers between devices: 153 us -> none  [on_device(): range_rows = lax.psum(range_part, 'col')]
  transfers between devices with their start and end apart: 7 -> 9, of which waited for: 6 -> 8; matrix products, arithmetic and copies ran while one was open for 3% -> 2% of each run, Pallas kernels for 0% -> 0%
where the time goes in v1:
time: 1080 us
  waiting for transfers between devices  647 us (60%)
  blocking collectives  210 us (19%)
  matrix products  149 us (14%)
  other arithmetic  49.1 us (5%)
  between operations  14.3 us (1%)
    ppermute x3, waiting for transfers between devices, sum_by_hops(): total = total + lax.ppermute(total, axis, swap)  361 us
    psum x1, blocking collectives, on_device(): lax.psum(jnp.dot(joined, basis_out, preferred_element_type=jnp.float32),...  150 us
    all_gather x1, waiting for transfers between devices, on_device(): full_acts = lax.all_gather(acts, 'col', axis=0, tiled=True)  94.1 us
    psum x1, waiting for transfers between devices, on_device(): core = lax.psum(core_part.astype(jnp.bfloat16), 'col')  74 us
    reduce_scatter x1, waiting for transfers between devices, on_device(): lax.psum_scatter(jnp.einsum('tqi,ij->tqj', rows, basis_in, preferred_elem...  51.3 us
    psum x1, blocking collectives, on_device(): reduced = lax.psum(reduced_part, 'row').astype(jnp.bfloat16)  39.9 us
    psum x1, waiting for transfers between devices, on_device(): mapped = lax.psum(mapped_part.astype(jnp.bfloat16), 'row')  34.7 us
    psum x1, waiting for transfers between devices, on_device(): lax.psum(projection_part.astype(jnp.bfloat16), 'row').astype(jnp.float32)  31.6 us
  transfers between devices with their start and end apart: 9, of which 8 were waited for; matrix products, arithmetic and copies ran while one was open for 2% of the time, Pallas kernels for 0%

profile of v1, /device:TPU:0, one launch (start us, length us, event | category | flops | bytes accessed | tf_op | source)
XLA Modules:
  0.0 1078.4 jit_solution(6995597473885565088)
XLA Ops:
  7.9 94.1 %all-gather.3.cloned.1.call-done = bf16[192,2,7168]{2,1,0:T(2,128)(2,1)} async-done(((bf16[24,2,7168]{2,1,0:T(2,128)(2,1)}), bf16[192,2,7168]{2,1,0:T(2,128)(2,1)}) %all-gather.3.cloned.1.call-update) | async-done | bytes 5505040 | tf_op jit(solution)/shard_map/all_gather | solution.py:16
  102.0 30.9 %fusion.4 = f32[192,2,3584]{2,0,1:T(8,128)} fusion(bf16[7168,3584]{1,0:T(8,128)(2,1)} %param.8, bf16[192,2,7168]{2,1,0:T(2,128)(2,1)} %all-gather.3.cloned.1.call-done), kind=kOutput, calls=%fused_computation.5 | convolution fusion | flops 19730006016 | bytes 62390272 | tf_op jit(solution)/shard_map/tqi,ij->tqj/dot_general | solution.py:19
  133.0 51.3 %reduce-scatter.2.cloned.1.call-done = f32[48,2,3584]{2,0,1:T(8,128)} async-done(((f32[192,2,3584]{2,0,1:T(8,128)}), f32[48,2,3584]{2,0,1:T(8,128)}) %reduce-scatter.2.cloned.1.call-update) | async-done | bytes 1376272 | tf_op jit(solution)/shard_map/reduce_scatter | solution.py:18
  184.3 2.3 convert_element_type.31
  186.7 8.0 all_gather.9
  195.0 6.2 fusion.18
  201.2 150.4 %all-reduce.11 = bf16[456,2048]{1,0:T(8,128)(2,1)S(1)} all-reduce(f32[456,2048]{1,0:T(8,128)} %fusion.18), channel_id=1, replica_groups=mesh['row'=4,'col'=8] {'col'}, use_global_device_ids=true, to_apply=%region_0.0 | all-reduce | flops 933888 | bytes 5603328 | tf_op jit(solution)/shard_map/psum | solution.py:29
  351.8 2.4 reshape.22
  354.1 16.6 %convert_element_type.32 = f32[3584,2048]{1,0:T(8,128)} convert(bf16[3584,2048]{1,0:T(8,128)(2,1)} %param.10) | non-fusion elementwise | flops 7340032 | bytes 44040192 | tf_op jit(solution)/shard_map/convert_element_type | solution.py:41
  370.8 22.4 %divide_convert_fusion = bf16[2,3584,2048]{2,1,0:T(8,128)(2,1)} fusion(f32[3584,2048]{1,0:T(8,128)} %convert_element_type.32, bf16[192,2,3584]{2,0,1:T(8,128)(2,1)} %all-gather.5.cloned.1.call-done, bf16[192,2,2048]{2,1,0:T(2,128)(2,1)S(1)} %copy-done.3), kind=kOutput, calls=%fused_computation | convolution fusion | flops 5666504704 | bytes 63045632 | tf_op jit(solution)/shard_map/tqj,tqp->qjp/dot_general | solution.py:35
  393.2 14.3 %convolution_bitcast_fusion = f32[2,72,3584]{2,1,0:T(8,128)S(1)} fusion(bf16[2,3584,2048]{2,1,0:T(8,128)(2,1)} %divide_convert_fusion, bf16[456,2048]{1,0:T(8,128)(2,1)} %copy-done.2), kind=kOutput, calls=%fused_computation.8 | convolution fusion | flops 2113929216 | bytes 31719424 | tf_op jit(solution)/shard_map/qjp,sp->qsj/dot_general | solution.py:42
  407.5 39.9 %all-reduce.12 = bf16[2,72,3584]{2,1,0:T(8,128)(2,1)S(1)} all-reduce(f32[2,72,3584]{2,1,0:T(8,128)S(1)} %convolution_bitcast_fusion), channel_id=1, replica_groups=mesh['row'=4,'col'=8] {'row'}, use_global_device_ids=true, to_apply=%region_2.0 | all-reduce | flops 516096 | bytes 3096576 | tf_op jit(solution)/shard_map/psum | solution.py:43
  447.5 26.5 %fusion.2 = f32[2,72,7168]{2,1,0:T(8,128)} fusion(bf16[7168,3584]{1,0:T(8,128)(2,1)} %param.8, bf16[2,72,3584]{2,1,0:T(8,128)(2,1)S(1)} %all-reduce.12), kind=kOutput, calls=%fused_computation.3 | convolution fusion | flops 7398752256 | bytes 56541184 | tf_op jit(solution)/shard_map/qsj,ij->qsi/dot_general | solution.py:44
  474.0 92.0 %collective-permute-done = f32[2,72,7168]{2,1,0:T(8,128)S(1)} collective-permute-done((f32[2,72,7168]{2,1,0:T(8,128)}, f32[2,72,7168]{2,1,0:T(8,128)S(1)}, u32[]{:S(2)}, u32[]{:S(2)}) %collective-permute-start) | collective-permute-done | bytes 4128800 | tf_op jit(solution)/shard_map/ppermute | solution.py:11
  566.0 2.7 add.34
  569.1 90.7 %collective-permute-done.1 = f32[2,72,7168]{2,1,0:T(8,128)S(1)} collective-permute-done((f32[2,72,7168]{2,1,0:T(8,128)S(1)}, f32[2,72,7168]{2,1,0:T(8,128)S(1)}, u32[]{:S(2)}, u32[]{:S(2)}) %collective-permute-start.1) | collective-permute-done | bytes 4128800 | tf_op jit(solution)/shard_map/ppermute | solution.py:11
  660.3 1.5 collective-permute-start.2
  661.8 178.0 %collective-permute-done.2 = f32[2,72,7168]{2,1,0:T(8,128)S(1)} collective-permute-done((f32[2,72,7168]{2,1,0:T(8,128)S(1)}, f32[2,72,7168]{2,1,0:T(8,128)S(1)}, u32[]{:S(2)}, u32[]{:S(2)}) %collective-permute-start.2) | collective-permute-done | bytes 4128800 | tf_op jit(solution)/shard_map/ppermute | solution.py:11
  840.3 2.0 copy-done
  842.3 4.0 fusion.26
  846.3 11.6 %psum.44 = f32[2,72,72]{1,2,0:T(8,128)S(1)} all-reduce(f32[2,72,72]{1,2,0:T(8,128)S(1)} %fusion.26), channel_id=1, replica_groups=mesh['row'=4,'col'=8] {'row'}, use_global_device_ids=true, to_apply=%region_3.0 | all-reduce | flops 10368 | bytes 82944 | tf_op jit(solution)/shard_map/psum | solution.py:47
  858.0 13.2 %custom-call.7 = f32[2,72,72]{2,1,0:T(8,128)S(1)} custom-call(f32[2,72,72]{2,1,0:T(8,128)S(1)} %fusion.24), custom_call_target="Cholesky" | custom-call | tf_op jit(solution)/shard_map/jit(cholesky)/cholesky | solution.py:48
  871.5 11.1 %custom-call.8 = f32[2,1,72,72]{2,3,1,0:T(8,128)S(1)} custom-call(f32[2,1,72,72]{3,2,1,0:T(8,128)S(1)} %select_bitcast_fusion), custom_call_target="InvertDiagBlocksLowerTriangular" | custom-call | tf_op jit(solution)/shard_map/triangular_solve | solution.py:49
  882.6 5.3 fusion.22
  888.0 2.0 copy-done.1
  889.9 19.0 %fusion.7 = bf16[2,72,3584]{2,1,0:T(8,128)(2,1)} fusion(bf16[7168,3584]{1,0:T(8,128)(2,1)} %param.8, f32[2,72,7168]{2,1,0:T(8,128)S(1)} %fusion.22), kind=kOutput, calls=%fused_computation.9 | convolution fusion | flops 7400300544 | bytes 56541184 | tf_op jit(solution)/shard_map/qsi,ij->qsj/dot_general | solution.py:50
  909.0 34.7 %all-reduce.6.cloned.1.call-done = bf16[2,72,3584]{2,1,0:T(8,128)(2,1)} async-done(((bf16[2,72,3584]{2,1,0:T(8,128)(2,1)}), bf16[2,72,3584]{2,1,0:T(8,128)(2,1)}) %all-reduce.6.cloned.1.call-update) | async-done | bytes 1032208 | tf_op jit(solution)/shard_map/psum | solution.py:53
  943.8 15.7 %convolution_convert_fusion = bf16[2,72,2048]{2,1,0:T(8,128)(2,1)} fusion(bf16[2,72,3584]{2,1,0:T(8,128)(2,1)} %all-reduce.6.cloned.1.call-done, bf16[2,3584,2048]{2,1,0:T(8,128)(2,1)} %divide_convert_fusion), kind=kOutput, calls=%fused_computation.12 | convolution fusion | flops 2114224128 | bytes 30982144 | tf_op jit(solution)/shard_map/qsj,qjp->qsp/dot_general | solution.py:54
  959.6 74.0 %all-reduce.8.cloned.1.call-done = bf16[2,72,2048]{2,1,0:T(8,128)(2,1)} async-done(((bf16[2,72,2048]{2,1,0:T(8,128)(2,1)}), bf16[2,72,2048]{2,1,0:T(8,128)(2,1)}) %all-reduce.8.cloned.1.call-update) | async-done | bytes 589840 | tf_op jit(solution)/shard_map/psum | solution.py:55
  1033.5 4.6 fusion.14
  1038.2 31.6 %all-reduce.10.cloned.1.call-done = bf16[2,72,1024]{2,1,0:T(8,128)(2,1)} async-done(((bf16[2,72,1024]{2,1,0:T(8,128)(2,1)}), bf16[2,72,1024]{2,1,0:T(8,128)(2,1)}) %all-reduce.10.cloned.1.call-update) | async-done | bytes 294928 | tf_op jit(solution)/shard_map/psum | solution.py:57
  1069.8 1.8 convert_element_type.39
  (36 shorter events, 3.3 us)
Async XLA Ops:
  7.2 94.9 %all-gather.3.cloned.1.call-start = ((), (), s32[]{:S(2)}) async-start(), calls=%async_computation.1 | async-start | bytes 6193152 | tf_op jit(solution)/shard_map/all_gather | solution.py:16
  7.9 176.4 %reduce-scatter.2.cloned.1.call-start = ((), (), s32[]{:S(2)}) async-start(), calls=%async_computation.2 | async-start | bytes 6881280 | tf_op jit(solution)/shard_map/reduce_scatter | solution.py:18
  133.0 53.7 %copy-start.4 = (bf16[48,2,1024]{2,1,0:T(2,128)(2,1)S(1)}, bf16[48,2,1024]{2,1,0:T(2,128)(2,1)}, u32[]{:S(2)}) copy-start(bf16[48,2,1024]{2,1,0:T(2,128)(2,1)} %param.7) | copy-start | bytes 589828
  133.0 62.0 %copy-start.5 = (bf16[72,1024]{1,0:T(8,128)(2,1)S(1)}, bf16[72,1024]{1,0:T(8,128)(2,1)}, u32[]{:S(2)}) copy-start(bf16[72,1024]{1,0:T(8,128)(2,1)} %param.11) | copy-start | bytes 442372
  133.0 237.8 %all-gather.5.cloned.1.call-start = ((), (), s32[]{:S(2)}) async-start(), calls=%async_computation.3 | async-start | bytes 3440640 | tf_op jit(solution)/shard_map/all_gather | solution.py:37
  186.6 757.2 %all-reduce.6.cloned.1.call-start = ((), (), s32[]{:S(2)}) async-start(), calls=%async_computation.4 | async-start | bytes 2064384 | tf_op jit(solution)/shard_map/psum | solution.py:53
  351.6 19.2 %copy-start.2 = (bf16[456,2048]{1,0:T(8,128)(2,1)}, bf16[456,2048]{1,0:T(8,128)(2,1)S(1)}, u32[]{:S(2)}) copy-start(bf16[456,2048]{1,0:T(8,128)(2,1)S(1)} %all-reduce.11) | copy-start | bytes 5603332
  354.1 16.7 %copy-start.3 = (bf16[192,2,2048]{2,1,0:T(2,128)(2,1)S(1)}, bf16[192,2,2048]{2,1,0:T(2,128)(2,1)}, u32[]{:S(2)}) copy-start(bf16[192,2,2048]{2,1,0:T(2,128)(2,1)} %reshape.22) | copy-start | bytes 4718596
  474.0 92.0 %collective-permute-start = (f32[2,72,7168]{2,1,0:T(8,128)}, f32[2,72,7168]{2,1,0:T(8,128)S(1)}, u32[]{:S(2)}, u32[]{:S(2)}) collective-permute-start(f32[2,72,7168]{2,1,0:T(8,128)} %fusion.2), channel_id=1, source_target_pairs={{0,1},{1,0},{2,3},{3,2},{4,5},{5,4},{6,7},{7,6},{8,9},{9,8},{10,11... | collective-permute-start | bytes 12386312 | tf_op jit(solution)/shard_map/ppermute | solution.py:11
  568.7 91.0 %collective-permute-start.1 = (f32[2,72,7168]{2,1,0:T(8,128)S(1)}, f32[2,72,7168]{2,1,0:T(8,128)S(1)}, u32[]{:S(2)}, u32[]{:S(2)}) collective-permute-start(f32[2,72,7168]{2,1,0:T(8,128)S(1)} %add.34), channel_id=1, source_target_pairs={{0,2},{1,3},{2,0},{3,1},{4,6},{5,7},{6,4},{7,5},{8,10},{9,11},{10,... | collective-permute-start | bytes 12386312 | tf_op jit(solution)/shard_map/ppermute | solution.py:11
  660.3 179.5 %collective-permute-start.2 = (f32[2,72,7168]{2,1,0:T(8,128)S(1)}, f32[2,72,7168]{2,1,0:T(8,128)S(1)}, u32[]{:S(2)}, u32[]{:S(2)}) collective-permute-start(f32[2,72,7168]{2,1,0:T(8,128)S(1)} %add.35), channel_id=1, source_target_pairs={{0,4},{1,5},{2,6},{3,7},{4,0},{5,1},{6,2},{7,3},{8,12},{9,13},{10,... | collective-permute-start | bytes 12386312 | tf_op jit(solution)/shard_map/ppermute | solution.py:11
  840.3 2.0 copy-start
  888.0 2.0 copy-start.1
  909.0 124.6 %all-reduce.8.cloned.1.call-start = ((), (), s32[]{:S(2)}) async-start(), calls=%async_computation.5 | async-start | bytes 1179648 | tf_op jit(solution)/shard_map/psum | solution.py:55
  959.5 110.3 %all-reduce.10.cloned.1.call-start = ((), (), s32[]{:S(2)}) async-start(), calls=%async_computation.6 | async-start | bytes 589824 | tf_op jit(solution)/shard_map/psum | solution.py:57
Sparse Core Ops, SparseCore 0:
  10.2 91.8 all-gather.2
  133.1 51.1 reduce-scatter.1
  186.7 26.2 all-gather.4
  909.1 34.6 all-reduce.5
  959.6 73.8 all-reduce.7
  1038.3 31.3 all-reduce.9
